TPU v7x, 32 devices: a whole 2x2x4 slice. The times are simulated.
32 devices in a mesh: fsdp: 2 (over y), ctx: 4 (over z), tp: 4 (over x, core).
Axes of the slice: x: 2, y: 2, z: 4, core: 2. Of those that a mesh axis runs over, the one named last changes fastest.
Arguments:
- tokens: bfloat16 [4, 4, 1024, 1024], P(None, 'fsdp', 'ctx', 'tp'), may hold values from -6 to 6
- skip_tokens: bfloat16 [4, 4, 1024, 1024], P(None, 'fsdp', 'ctx', 'tp'), may hold values from -6 to 6
- merger_weight: bfloat16 [1024, 2, 1024], P(('fsdp', 'ctx'), None, 'tp'), may hold values from -0.125 to 0.125
- merger_bias: float32 [1024], P(('fsdp', 'ctx', 'tp')), may hold values from -3 to 3
- first_gain: float32 [1024], P(('fsdp', 'ctx', 'tp')), may hold values from 0.25 to 1.75
- first_shift: float32 [1024], P(('fsdp', 'ctx', 'tp')), may hold values from -2 to 2
- attend_weight: bfloat16 [1024, 3, 1024], P(('fsdp', 'ctx'), None, 'tp'), may hold values from -0.25 to 0.25
- output_weight: bfloat16 [1024, 1024], P(('fsdp', 'ctx'), 'tp'), may hold values from -0.75 to 0.75
- output_bias: float32 [1024], P(('fsdp', 'ctx', 'tp')), may hold values from -2 to 2
- second_gain: float32 [1024], P(('fsdp', 'ctx', 'tp')), may hold values from 0.25 to 1.75
- second_shift: float32 [1024], P(('fsdp', 'ctx', 'tp')), may hold values from -2 to 2
- expand_weight: bfloat16 [1024, 4096], P(('fsdp', 'ctx'), 'tp'), may hold values from -0.1875 to 0.1875
- widen_bias: float32 [4096], P(('fsdp', 'ctx', 'tp')), may hold values from -3 to 3
- shrink_weight: bfloat16 [1024, 4096], P(('fsdp', 'ctx'), 'tp'), may hold values from -0.125 to 0.125
- shrink_bias: float32 [1024], P(('fsdp', 'ctx', 'tp')), may hold values from -2 to 2
- live_slots: int32 [4, 4], P(None, 'fsdp'), may hold values from 0 to 1, as said below
- cotangent: bfloat16 [4, 4, 1024, 1024], P(None, 'fsdp', ('ctx', 'tp')), may hold values from -6 to 6
Outputs:
- layer_out: bfloat16 [4, 4, 1024, 1024], P(None, 'fsdp', ('ctx', 'tp'))
- grad_tokens: float32 [4, 4, 1024, 1024], P(None, 'fsdp', 'ctx', 'tp')
- grad_skip: float32 [4, 4, 1024, 1024], P(None, 'fsdp', 'ctx', 'tp')
- weight_merger: float32 [1024, 2, 1024], P(('fsdp', 'ctx'), None, 'tp')
- bias_merger: float32 [1024], P(('fsdp', 'ctx', 'tp'))
- gain_first: float32 [1024], P(('fsdp', 'ctx', 'tp'))
- shift_first: float32 [1024], P(('fsdp', 'ctx', 'tp'))
- weight_attend: float32 [1024, 3, 1024], P(('fsdp', 'ctx'), None, 'tp')
- weight_output: float32 [1024, 1024], P(('fsdp', 'ctx'), 'tp')
- bias_output: float32 [1024], P(('fsdp', 'ctx', 'tp'))
- gain_second: float32 [1024], P(('fsdp', 'ctx', 'tp'))
- shift_second: float32 [1024], P(('fsdp', 'ctx', 'tp'))
- weight_expand: float32 [1024, 4096], P(('fsdp', 'ctx'), 'tp')
- bias_expand: float32 [4096], P(('fsdp', 'ctx', 'tp'))
- weight_shrink: float32 [1024, 4096], P(('fsdp', 'ctx'), 'tp')
- bias_shrink: float32 [1024], P(('fsdp', 'ctx', 'tp'))
Inputs may be any that keep to these rules, and one draw needn't show every extreme that they name: `live_slots`: in every micro-batch but the last exactly one of the 4 slots is empty (0), in the last exactly two; the empty slots lie anywhere.
All inputs are finite; a program needn't handle non-finite values.
Results may differ from a plain program's by a relative error of at most 0.017.
Values may be sent and summed in bfloat16 or wider, within the bound.
No kernel may reach another device: no remote copies, remote signals or barrier semaphores. Data moves between devices by JAX's collectives and lax.ppermute only.
A program may use at most 256 MiB of HBM per device.

v0:
```python
import jax
import jax.numpy as jnp
from jax import lax
from jax.sharding import PartitionSpec as P

HD = 64
EPSILON = 1e-05


def layer_norm(matrix, scales, shifts):
    center = matrix - jnp.mean(matrix, axis=-1, keepdims=True)
    spread = jnp.mean(center * center, axis=-1, keepdims=True)
    return center * lax.rsqrt(spread + EPSILON) * scales + shifts


def gelu_exact(matrix):
    return jax.nn.gelu(matrix, approximate=False)


def fetch(merger_part, attend_part, output_part, expand_part, shrink_part):
    return (
        lax.all_gather(merger_part, ("fsdp", "ctx"), axis=0, tiled=True),
        lax.all_gather(attend_part, ("fsdp", "ctx"), axis=0, tiled=True),
        lax.all_gather(output_part, ("fsdp", "ctx"), axis=0, tiled=True),
        lax.all_gather(expand_part, ("fsdp", "ctx"), axis=0, tiled=True),
        lax.all_gather(shrink_part, ("fsdp", "ctx"), axis=0, tiled=True),
    )


def spread_rows(block):
    return lax.all_gather(block, "tp", axis=1, tiled=True)


def fold_rows(block):
    return lax.psum_scatter(block, "tp", scatter_dimension=1, tiled=True)


def reduce_weights(parts):
    return (
        lax.psum_scatter(parts[0], ("fsdp", "ctx"), scatter_dimension=0, tiled=True),
        lax.psum_scatter(parts[1], ("fsdp", "ctx"), scatter_dimension=0, tiled=True),
        lax.psum_scatter(parts[2], ("fsdp", "ctx"), scatter_dimension=0, tiled=True),
        lax.psum_scatter(parts[3], ("fsdp", "ctx"), scatter_dimension=0, tiled=True),
        lax.psum_scatter(parts[4], ("fsdp", "ctx"), scatter_dimension=0, tiled=True),
    )


def micro_step(weights, vectors, tokens_now, skips_now, live_now, cot_now, tensor_rank):
    merger_full, attend_full, output_full, expand_full, shrink_full = weights
    (
        merger_bias,
        first_gain,
        first_shift,
        output_bias,
        second_gain,
        second_shift,
        shrink_bias,
        widen_bias,
    ) = vectors
    groups = tokens_now.shape[0]
    local_len = tokens_now.shape[1]
    heads_dev = attend_full.shape[2] // HD
    hidden = expand_full.shape[1]
    scaling = HD ** (-0.5)
    stacked = jnp.stack([tokens_now, skips_now], axis=2)
    joined = (
        fold_rows(
            jnp.einsum("stci,oci->sto", stacked, merger_full, preferred_element_type=jnp.float32)
        )
        + merger_bias
    )
    normed, first_pull = jax.vjp(layer_norm, joined, first_gain, first_shift)
    normed_all = spread_rows(normed.astype(jnp.bfloat16))
    project = jnp.einsum(
        "std,dcj->stcj", normed_all, attend_full, preferred_element_type=jnp.float32
    ).astype(jnp.bfloat16)
    key_rows, value_rows = (
        lax.all_gather(project[:, :, 1], "ctx", axis=1, tiled=True),
        lax.all_gather(project[:, :, 2], "ctx", axis=1, tiled=True),
    )
    seq_len = key_rows.shape[1]
    query_heads = project[:, :, 0].reshape(groups, local_len, heads_dev, HD)
    key_heads = key_rows.reshape(groups, seq_len, heads_dev, HD)
    value_heads = value_rows.reshape(groups, seq_len, heads_dev, HD)
    scores = (
        jnp.einsum("sqhd,skhd->shqk", query_heads, key_heads, preferred_element_type=jnp.float32)
        * scaling
    )
    row_peak = jnp.max(scores, axis=-1, keepdims=True)
    logsum = row_peak + jnp.log(jnp.sum(jnp.exp(scores - row_peak), axis=-1, keepdims=True))
    probs_low = jnp.exp(scores - logsum).astype(jnp.bfloat16)
    attended = jnp.einsum(
        "shqk,skhd->sqhd", probs_low, value_heads, preferred_element_type=jnp.float32
    )
    attended = attended.astype(jnp.bfloat16).reshape(groups, local_len, heads_dev * HD)
    second = (
        joined
        + fold_rows(
            jnp.einsum("sti,oi->sto", attended, output_full, preferred_element_type=jnp.float32)
        )
        + output_bias
    )
    normed_two, second_pull = jax.vjp(layer_norm, second, second_gain, second_shift)
    normed_two_all = spread_rows(normed_two.astype(jnp.bfloat16))
    bias_slice = lax.dynamic_slice_in_dim(widen_bias, tensor_rank * hidden, hidden)
    widened_hidden = (
        jnp.einsum("std,df->stf", normed_two_all, expand_full, preferred_element_type=jnp.float32)
        + bias_slice
    )
    activated, gelu_pull = jax.vjp(gelu_exact, widened_hidden)
    activated_low = activated.astype(jnp.bfloat16)
    result = (
        second
        + fold_rows(
            jnp.einsum(
                "stf,of->sto", activated_low, shrink_full, preferred_element_type=jnp.float32
            )
        )
        + shrink_bias
    )
    live_mask = live_now.astype(jnp.float32)[:, None, None]
    layer_out = (result * live_mask).astype(jnp.bfloat16)
    upstream = cot_now.astype(jnp.float32) * live_mask
    grad_shrink_bias = jnp.sum(upstream, axis=(0, 1))
    branch_low = spread_rows(upstream.astype(jnp.bfloat16))
    grad_shrink = jnp.einsum(
        "sto,stf->of", branch_low, activated_low, preferred_element_type=jnp.float32
    )
    grad_activated = jnp.einsum(
        "sto,of->stf", branch_low, shrink_full, preferred_element_type=jnp.float32
    )
    grad_expanded = gelu_pull(grad_activated)[0].astype(jnp.bfloat16)
    grad_expand_bias = jnp.sum(grad_expanded, axis=(0, 1), dtype=jnp.float32)
    grad_expand = jnp.einsum(
        "std,stf->df", normed_two_all, grad_expanded, preferred_element_type=jnp.float32
    )
    grad_normed_two = fold_rows(
        jnp.einsum("stf,df->std", grad_expanded, expand_full, preferred_element_type=jnp.float32)
    )
    grad_second_norm, grad_second_gain, grad_second_shift = second_pull(grad_normed_two)
    grad_second = upstream + grad_second_norm
    grad_output_bias = jnp.sum(grad_second, axis=(0, 1))
    attn_low = spread_rows(grad_second.astype(jnp.bfloat16))
    grad_output = jnp.einsum("sto,sti->oi", attn_low, attended, preferred_element_type=jnp.float32)
    grad_attended = jnp.einsum(
        "sto,oi->sti", attn_low, output_full, preferred_element_type=jnp.float32
    )
    grad_attended = grad_attended.astype(jnp.bfloat16).reshape(groups, local_len, heads_dev, HD)
    scores_again = (
        jnp.einsum("sqhd,skhd->shqk", query_heads, key_heads, preferred_element_type=jnp.float32)
        * scaling
    )
    probs = jnp.exp(scores_again - logsum)
    grad_probs = jnp.einsum(
        "sqhd,skhd->shqk", grad_attended, value_heads, preferred_element_type=jnp.float32
    )
    row_inner = jnp.sum(probs * grad_probs, axis=-1, keepdims=True)
    grad_scores = (probs * (grad_probs - row_inner)).astype(jnp.bfloat16)
    grad_queries = (
        jnp.einsum("shqk,skhd->sqhd", grad_scores, key_heads, preferred_element_type=jnp.float32)
        * scaling
    )
    probs_again = probs.astype(jnp.bfloat16)
    key_terms = (
        jnp.einsum("shqk,sqhd->skhd", grad_scores, query_heads, preferred_element_type=jnp.float32)
        * scaling
    )
    value_terms = jnp.einsum(
        "shqk,sqhd->skhd", probs_again, grad_attended, preferred_element_type=jnp.float32
    )
    grad_keys, grad_values = (
        lax.psum_scatter(
            key_terms.reshape(groups, seq_len, heads_dev * HD).astype(jnp.bfloat16),
            "ctx",
            scatter_dimension=1,
            tiled=True,
        ).astype(jnp.float32),
        lax.psum_scatter(
            value_terms.reshape(groups, seq_len, heads_dev * HD).astype(jnp.bfloat16),
            "ctx",
            scatter_dimension=1,
            tiled=True,
        ).astype(jnp.float32),
    )
    grad_project = jnp.stack(
        [
            grad_queries.reshape(groups, local_len, heads_dev * HD).astype(jnp.bfloat16),
            grad_keys.astype(jnp.bfloat16),
            grad_values.astype(jnp.bfloat16),
        ],
        axis=2,
    )
    grad_attend = jnp.einsum(
        "std,stcj->dcj", normed_all, grad_project, preferred_element_type=jnp.float32
    )
    grad_normed = fold_rows(
        jnp.einsum("stcj,dcj->std", grad_project, attend_full, preferred_element_type=jnp.float32)
    )
    grad_first_norm, gradient_leading_gain, grad_first_shift = first_pull(grad_normed)
    grad_joined = grad_second + grad_first_norm
    grad_merger_bias = jnp.sum(grad_joined, axis=(0, 1))
    joined_low = spread_rows(grad_joined.astype(jnp.bfloat16))
    grad_merger = jnp.einsum(
        "sto,stci->oci", joined_low, stacked, preferred_element_type=jnp.float32
    )
    grad_stacked = jnp.einsum(
        "sto,oci->stci", joined_low, merger_full, preferred_element_type=jnp.float32
    )
    expand_whole = lax.dynamic_update_slice_in_dim(
        jnp.zeros((widen_bias.shape[0],), jnp.float32), grad_expand_bias, tensor_rank * hidden, 0
    )
    weight_part = (grad_merger, grad_attend, grad_output, grad_expand, grad_shrink)
    vector_portion = (
        grad_merger_bias,
        gradient_leading_gain,
        grad_first_shift,
        grad_output_bias,
        grad_second_gain,
        grad_second_shift,
        grad_shrink_bias,
        expand_whole,
    )
    return (layer_out, grad_stacked[:, :, 0], grad_stacked[:, :, 1], weight_part, vector_portion)


def on_device(
    tokens,
    skip_tokens,
    merger_weight,
    merger_bias,
    first_gain,
    first_shift,
    attend_weight,
    output_weight,
    output_bias,
    second_gain,
    second_shift,
    expand_weight,
    widen_bias,
    shrink_weight,
    shrink_bias,
    live_slots,
    cotangent,
):
    tensor_rank = lax.axis_index("tp")
    vectors = (
        lax.all_gather(merger_bias, ("fsdp", "ctx", "tp"), axis=0, tiled=True),
        lax.all_gather(first_gain, ("fsdp", "ctx", "tp"), axis=0, tiled=True),
        lax.all_gather(first_shift, ("fsdp", "ctx", "tp"), axis=0, tiled=True),
        lax.all_gather(output_bias, ("fsdp", "ctx", "tp"), axis=0, tiled=True),
        lax.all_gather(second_gain, ("fsdp", "ctx", "tp"), axis=0, tiled=True),
        lax.all_gather(second_shift, ("fsdp", "ctx", "tp"), axis=0, tiled=True),
        lax.all_gather(shrink_bias, ("fsdp", "ctx", "tp"), axis=0, tiled=True),
        lax.all_gather(widen_bias, ("fsdp", "ctx", "tp"), axis=0, tiled=True),
    )
    batches = tokens.shape[0]
    outs_list = []
    token_list = []
    skip_list = []
    weight_totals = None
    vector_totals = None
    for batch_index in range(batches):
        current = fetch(merger_weight, attend_weight, output_weight, expand_weight, shrink_weight)
        layer_out, grad_one, gradient_remaining, weight_part, vector_portion = micro_step(
            current,
            vectors,
            tokens[batch_index],
            skip_tokens[batch_index],
            live_slots[batch_index],
            cotangent[batch_index],
            tensor_rank,
        )
        if weight_totals is None:
            weight_totals = weight_part
            vector_totals = vector_portion
        else:
            weight_totals = tuple(
                (former + latter for former, latter in zip(weight_totals, weight_part))
            )
            vector_totals = tuple(
                (former + latter for former, latter in zip(vector_totals, vector_portion))
            )
        outs_list.append(layer_out)
        token_list.append(grad_one)
        skip_list.append(gradient_remaining)
    weight_totals = reduce_weights(weight_totals)
    vector_grads = (
        lax.psum_scatter(vector_totals[0], ("fsdp", "ctx", "tp"), scatter_dimension=0, tiled=True),
        lax.psum_scatter(vector_totals[1], ("fsdp", "ctx", "tp"), scatter_dimension=0, tiled=True),
        lax.psum_scatter(vector_totals[2], ("fsdp", "ctx", "tp"), scatter_dimension=0, tiled=True),
        lax.psum_scatter(vector_totals[3], ("fsdp", "ctx", "tp"), scatter_dimension=0, tiled=True),
        lax.psum_scatter(vector_totals[4], ("fsdp", "ctx", "tp"), scatter_dimension=0, tiled=True),
        lax.psum_scatter(vector_totals[5], ("fsdp", "ctx", "tp"), scatter_dimension=0, tiled=True),
        lax.psum_scatter(vector_totals[6], ("fsdp", "ctx", "tp"), scatter_dimension=0, tiled=True),
        lax.psum_scatter(vector_totals[7], ("fsdp", "ctx", "tp"), scatter_dimension=0, tiled=True),
    )
    return (
        jnp.stack(outs_list, axis=0),
        jnp.stack(token_list, axis=0),
        jnp.stack(skip_list, axis=0),
        weight_totals[0],
        vector_grads[0],
        vector_grads[1],
        vector_grads[2],
        weight_totals[1],
        weight_totals[2],
        vector_grads[3],
        vector_grads[4],
        vector_grads[5],
        weight_totals[3],
        vector_grads[7],
        weight_totals[4],
        vector_grads[6],
    )


def solution(mesh):
    placed = (
        P(None, "fsdp", "ctx", "tp"),
        P(None, "fsdp", "ctx", "tp"),
        P(("fsdp", "ctx"), None, "tp"),
        P(("fsdp", "ctx", "tp")),
        P(("fsdp", "ctx", "tp")),
        P(("fsdp", "ctx", "tp")),
        P(("fsdp", "ctx"), None, "tp"),
        P(("fsdp", "ctx"), "tp"),
        P(("fsdp", "ctx", "tp")),
        P(("fsdp", "ctx", "tp")),
        P(("fsdp", "ctx", "tp")),
        P(("fsdp", "ctx"), "tp"),
        P(("fsdp", "ctx", "tp")),
        P(("fsdp", "ctx"), "tp"),
        P(("fsdp", "ctx", "tp")),
        P(None, "fsdp"),
        P(None, "fsdp", ("ctx", "tp"), None),
    )
    return jax.shard_map(
        on_device,
        mesh=mesh,
        in_specs=placed,
        out_specs=(
            P(None, "fsdp", ("ctx", "tp"), None),
            P(None, "fsdp", "ctx", "tp"),
            P(None, "fsdp", "ctx", "tp"),
            P(("fsdp", "ctx"), None, "tp"),
            P(("fsdp", "ctx", "tp")),
            P(("fsdp", "ctx", "tp")),
            P(("fsdp", "ctx", "tp")),
            P(("fsdp", "ctx"), None, "tp"),
            P(("fsdp", "ctx"), "tp"),
            P(("fsdp", "ctx", "tp")),
            P(("fsdp", "ctx", "tp")),
            P(("fsdp", "ctx", "tp")),
            P(("fsdp", "ctx"), "tp"),
            P(("fsdp", "ctx", "tp")),
            P(("fsdp", "ctx"), "tp"),
            P(("fsdp", "ctx", "tp")),
        ),
        check_vma=False,
    )
```

profile of v0, /device:TPU:0, one launch (start us, length us, event | category | flops | bytes accessed | tf_op | source)
XLA Modules:
  0.0 2147.7 jit_solution(7706245499468301437)
XLA Ops:
  10.6 43.0 %all-gather.42.cloned.1.call-done = bf16[1024,2,256]{2,0,1:T(8,128)(2,1)} async-done(((bf16[128,2,256]{2,0,1:T(8,128)(2,1)}), bf16[1024,2,256]{2,0,1:T(8,128)(2,1)}) %all-gather.42.cloned.1.call-update) | async-done | bytes 1048592 | tf_op jit(solution)/shard_map/all_gather | solution.py:22
  66.0 38.9 %all-reduce.16 = (f32[1024]{0:T(1024)S(1)}, f32[1024]{0:T(1024)S(1)}, f32[1024]{0:T(1024)S(1)}, f32[1024]{0:T(1024)S(1)}, f32[1024]{0:T(1024)S(1)}, /*index=5*/f32[1024]{0:T(1024)S(1)}) all-reduce(f32[1024]{0:T(1024)S(1)} %dynamic-update-slice.3, ...), channel_id=1, replica_groups=mesh['fsdp'=2,'ctx'=4,'tp'=4] {'fsdp','ctx','tp'}, use_global_device_ids=true, to_apply=%add | all-reduce | flops 6144 | bytes 49152
  122.3 33.8 %reduce-scatter.46.cloned.1.call-done = f32[2,64,1024]{2,1,0:T(8,128)} async-done(((f32[2,256,1024]{2,1,0:T(8,128)}), f32[2,64,1024]{2,1,0:T(8,128)}) %reduce-scatter.46.cloned.1.call-update) | async-done | bytes 524304 | tf_op jit(solution)/shard_map/reduce_scatter | solution.py:35
  156.1 34.0 %reduce-scatter.52.cloned.1.call-done = f32[2,64,1024]{2,1,0:T(8,128)} async-done(((f32[2,256,1024]{2,1,0:T(8,128)}), f32[2,64,1024]{2,1,0:T(8,128)}) %reduce-scatter.52.cloned.1.call-update) | async-done | bytes 524304 | tf_op jit(solution)/shard_map/reduce_scatter | solution.py:35
  196.6 41.2 %all-gather.46.cloned.1.call-done = bf16[1024,3,256]{0,2,1:T(8,128)(2,1)} async-done(((bf16[128,3,256]{0,2,1:T(8,128)(2,1)}), bf16[1024,3,256]{0,2,1:T(8,128)(2,1)}) %all-gather.46.cloned.1.call-update) | async-done | bytes 1572880 | tf_op jit(solution)/shard_map/all_gather | solution.py:23
  315.2 34.9 %all_gather.146 = bf16[1024,256]{1,0:T(8,128)(2,1)S(1)} all-gather(bf16[128,256]{1,0:T(8,128)(2,1)S(1)} %copy-done.113), channel_id=1, replica_groups=mesh['fsdp'=2,'ctx'=4,'tp'=4] {'fsdp','ctx'}, dimensions={0}, use_global_device_ids=true | all-gather | bytes 589824 | tf_op jit(solution)/shard_map/all_gather | solution.py:24
  596.2 34.6 %reduce-scatter.48.cloned.1.call-done = f32[2,64,1024]{2,1,0:T(8,128)} async-done(((f32[2,256,1024]{2,1,0:T(8,128)}), f32[2,64,1024]{2,1,0:T(8,128)}) %reduce-scatter.48.cloned.1.call-update) | async-done | bytes 524304 | tf_op jit(solution)/shard_map/reduce_scatter | solution.py:35
  630.8 34.0 %reduce-scatter.54.cloned.1.call-done = f32[2,64,1024]{2,1,0:T(8,128)} async-done(((f32[2,256,1024]{2,1,0:T(8,128)}), f32[2,64,1024]{2,1,0:T(8,128)}) %reduce-scatter.54.cloned.1.call-update) | async-done | bytes 524304 | tf_op jit(solution)/shard_map/reduce_scatter | solution.py:35
  664.8 34.2 %reduce-scatter.36.cloned.1.call-done = f32[2,64,1024]{2,1,0:T(8,128)} async-done(((f32[2,256,1024]{2,1,0:T(8,128)}), f32[2,64,1024]{2,1,0:T(8,128)}) %reduce-scatter.36.cloned.1.call-update) | async-done | bytes 524304 | tf_op jit(solution)/shard_map/reduce_scatter | solution.py:35
  711.8 41.1 %all-gather.8 = f32[32,1,128]{2,1,0:T(1,128)S(1)} all-gather(f32[1,1,128]{2,1,0:T(1,128)S(1)} %bitcast.612), channel_id=1, replica_groups=mesh['fsdp'=2,'ctx'=4,'tp'=4] {'fsdp','ctx','tp'}, dimensions={0}, use_global_device_ids=true | all-gather | bytes 16896 | tf_op jit(solution)/shard_map/all_gather | solution.py:254
  855.1 38.8 %all-gather.52.cloned.1.call-done = bf16[1024,1024]{1,0:T(8,128)(2,1)} async-done(((bf16[128,1024]{1,0:T(8,128)(2,1)}), bf16[1024,1024]{1,0:T(8,128)(2,1)}) %all-gather.52.cloned.1.call-update) | async-done | bytes 2097168 | tf_op jit(solution)/shard_map/all_gather | solution.py:26
  983.5 32.9 %reduce-scatter.74.cloned.1.call-done = f32[2,64,1024]{2,1,0:T(8,128)} async-done(((f32[2,256,1024]{2,1,0:T(8,128)}), f32[2,64,1024]{2,1,0:T(8,128)}) %reduce-scatter.74.cloned.1.call-update) | async-done | bytes 524304 | tf_op jit(solution)/shard_map/reduce_scatter | solution.py:35
  1016.4 34.0 %reduce-scatter.66.cloned.1.call-done = f32[2,64,1024]{2,1,0:T(8,128)} async-done(((f32[2,256,1024]{2,1,0:T(8,128)}), f32[2,64,1024]{2,1,0:T(8,128)}) %reduce-scatter.66.cloned.1.call-update) | async-done | bytes 524304 | tf_op jit(solution)/shard_map/reduce_scatter | solution.py:35
  1050.3 34.0 %reduce-scatter.58.cloned.1.call-done = f32[2,64,1024]{2,1,0:T(8,128)} async-done(((f32[2,256,1024]{2,1,0:T(8,128)}), f32[2,64,1024]{2,1,0:T(8,128)}) %reduce-scatter.58.cloned.1.call-update) | async-done | bytes 524304 | tf_op jit(solution)/shard_map/reduce_scatter | solution.py:35
  1422.7 34.7 %reduce-scatter.72.cloned.1.call-done = f32[2,64,1024]{2,1,0:T(8,128)} async-done(((f32[2,256,1024]{2,1,0:T(8,128)}), f32[2,64,1024]{2,1,0:T(8,128)}) %reduce-scatter.72.cloned.1.call-update) | async-done | bytes 524304 | tf_op jit(solution)/shard_map/reduce_scatter | solution.py:35
  1457.4 33.8 %reduce-scatter.64.cloned.1.call-done = f32[2,64,1024]{2,1,0:T(8,128)} async-done(((f32[2,256,1024]{2,1,0:T(8,128)}), f32[2,64,1024]{2,1,0:T(8,128)}) %reduce-scatter.64.cloned.1.call-update) | async-done | bytes 524304 | tf_op jit(solution)/shard_map/reduce_scatter | solution.py:35
  1491.2 34.2 %reduce-scatter.80.cloned.1.call-done = f32[2,64,1024]{2,1,0:T(8,128)} async-done(((f32[2,256,1024]{2,1,0:T(8,128)}), f32[2,64,1024]{2,1,0:T(8,128)}) %reduce-scatter.80.cloned.1.call-update) | async-done | bytes 524304 | tf_op jit(solution)/shard_map/reduce_scatter | solution.py:35
  1645.5 40.4 %all-reduce.15 = (f32[1024]{0:T(1024)S(1)}, f32[1024]{0:T(1024)S(1)}, f32[1024]{0:T(1024)S(1)}, f32[1024]{0:T(1024)S(1)}, f32[1024]{0:T(1024)S(1)}, /*index=5*/f...) all-reduce(f32[1024]{0:T(1024)S(1)} %dynamic-update-slice.9, ...), channel_id=1, replica_groups=mesh['fsdp'=2,'ctx'=4,'tp'=4] {'fsdp','ctx','tp'}, use_global_device_ids=true, to_apply=%add.6 | all-reduce | flops 12288 | bytes 98304
  1706.5 34.2 %reduce-scatter.56.cloned.1.call-done = f32[2,64,1024]{2,1,0:T(8,128)} async-done(((f32[2,256,1024]{2,1,0:T(8,128)}), f32[2,64,1024]{2,1,0:T(8,128)}) %reduce-scatter.56.cloned.1.call-update) | async-done | bytes 524304 | tf_op jit(solution)/shard_map/reduce_scatter | solution.py:35
  1752.1 59.7 %reduce-scatter.90.cloned.1.call-done = f32[128,2,256]{2,0,1:T(8,128)} async-done(((f32[1024,2,256]{2,0,1:T(8,128)}), f32[128,2,256]{2,0,1:T(8,128)}) %reduce-scatter.90.cloned.1.call-update) | async-done | bytes 262160 | tf_op jit(solution)/shard_map/reduce_scatter | solution.py:40
  1813.7 64.7 %reduce-scatter.94.cloned.1.call-done = f32[128,256]{1,0:T(8,128)} async-done(((f32[1024,256]{1,0:T(8,128)}), f32[128,256]{1,0:T(8,128)}) %reduce-scatter.94.cloned.1.call-update) | async-done | bytes 131088 | tf_op jit(solution)/shard_map/reduce_scatter | solution.py:42
  1878.3 91.6 %reduce-scatter.96.cloned.1.call-done = f32[128,1024]{1,0:T(8,128)} async-done(((f32[1024,1024]{1,0:T(8,128)}), f32[128,1024]{1,0:T(8,128)}) %reduce-scatter.96.cloned.1.call-update) | async-done | bytes 524304 | tf_op jit(solution)/shard_map/reduce_scatter | solution.py:43
  1969.9 91.7 %reduce-scatter.98.cloned.1.call-done = f32[128,1024]{1,0:T(8,128)} async-done(((f32[1024,1024]{1,0:T(8,128)}), f32[128,1024]{1,0:T(8,128)}) %reduce-scatter.98.cloned.1.call-update) | async-done | bytes 524304 | tf_op jit(solution)/shard_map/reduce_scatter | solution.py:44
  2061.6 79.3 %reduce-scatter.92.cloned.1.call-done = f32[128,3,256]{2,0,1:T(8,128)} async-done(((f32[1024,3,256]{2,0,1:T(8,128)}), f32[128,3,256]{2,0,1:T(8,128)}) %reduce-scatter.92.cloned.1.call-update) | async-done | bytes 393232 | tf_op jit(solution)/shard_map/reduce_scatter | solution.py:41
  (777 shorter events, 1056.6 us)
Async XLA Ops:
  64.5 190.4 %all-gather.54.cloned.1.call-start = ((), (), s32[]{:S(2)}) async-start(), calls=%async_computation.43 | async-start | bytes 1310720 | tf_op jit(solution)/shard_map/all_gather | solution.py:31
  278.0 194.9 %all-gather.104.cloned.1.call-start = ((), (), s32[]{:S(2)}) async-start(), calls=%async_computation.97 | async-start | bytes 1310720 | tf_op jit(solution)/shard_map/all_gather | solution.py:78
  296.4 206.6 %all-gather.102.cloned.1.call-start = ((), (), s32[]{:S(2)}) async-start(), calls=%async_computation.96 | async-start | bytes 1310720 | tf_op jit(solution)/shard_map/all_gather | solution.py:79
  296.9 236.5 %all-gather.92.cloned.1.call-start = ((), (), s32[]{:S(2)}) async-start(), calls=%async_computation.91 | async-start | bytes 1310720 | tf_op jit(solution)/shard_map/all_gather | solution.py:78
  315.1 248.3 %all-gather.90.cloned.1.call-start = ((), (), s32[]{:S(2)}) async-start(), calls=%async_computation.90 | async-start | bytes 1310720 | tf_op jit(solution)/shard_map/all_gather | solution.py:79
  350.1 246.2 %reduce-scatter.42.cloned.1.call-start = ((), (), s32[]{:S(2)}) async-start(), calls=%async_computation.44 | async-start | bytes 2621440 | tf_op jit(solution)/shard_map/reduce_scatter | solution.py:35
  388.4 242.4 %reduce-scatter.48.cloned.1.call-start = ((), (), s32[]{:S(2)}) async-start(), calls=%async_computation.49 | async-start | bytes 2621440 | tf_op jit(solution)/shard_map/reduce_scatter | solution.py:35
  449.6 215.2 %reduce-scatter.54.cloned.1.call-start = ((), (), s32[]{:S(2)}) async-start(), calls=%async_computation.54 | async-start | bytes 2621440 | tf_op jit(solution)/shard_map/reduce_scatter | solution.py:35
  571.3 196.4 %all-gather.60.cloned.1.call-start = ((), (), s32[]{:S(2)}) async-start(), calls=%async_computation.50 | async-start | bytes 1310720 | tf_op jit(solution)/shard_map/all_gather | solution.py:31
  709.7 200.8 %all-gather.78.cloned.1.call-start = ((), (), s32[]{:S(2)}) async-start(), calls=%async_computation.71 | async-start | bytes 1310720 | tf_op jit(solution)/shard_map/all_gather | solution.py:31
  710.3 218.6 %all-gather.72.cloned.1.call-start = ((), (), s32[]{:S(2)}) async-start(), calls=%async_computation.64 | async-start | bytes 1310720 | tf_op jit(solution)/shard_map/all_gather | solution.py:31
  711.0 236.2 %all-gather.66.cloned.1.call-start = ((), (), s32[]{:S(2)}) async-start(), calls=%async_computation.57 | async-start | bytes 1310720 | tf_op jit(solution)/shard_map/all_gather | solution.py:31
  711.8 269.8 %reduce-scatter.82.cloned.1.call-start = ((), (), s32[]{:S(2)}) async-start(), calls=%async_computation.79 | async-start | bytes 2621440 | tf_op jit(solution)/shard_map/reduce_scatter | solution.py:35
  1171.3 190.2 %reduce-scatter.78.cloned.1.call-start = ((), (), s32[]{:S(2)}) async-start(), calls=%async_computation.75 | async-start | bytes 1310720 | tf_op jit(solution)/shard_map/reduce_scatter | solution.py:178
  1179.7 209.9 %reduce-scatter.76.cloned.1.call-start = ((), (), s32[]{:S(2)}) async-start(), calls=%async_computation.74 | async-start | bytes 1310720 | tf_op jit(solution)/shard_map/reduce_scatter | solution.py:172
  1192.6 230.0 %reduce-scatter.88.cloned.1.call-start = ((), (), s32[]{:S(2)}) async-start(), calls=%async_computation.83 | async-start | bytes 2621440 | tf_op jit(solution)/shard_map/reduce_scatter | solution.py:35
  1225.2 232.2 %reduce-scatter.72.cloned.1.call-start = ((), (), s32[]{:S(2)}) async-start(), calls=%async_computation.69 | async-start | bytes 2621440 | tf_op jit(solution)/shard_map/reduce_scatter | solution.py:35
  1281.4 209.8 %reduce-scatter.64.cloned.1.call-start = ((), (), s32[]{:S(2)}) async-start(), calls=%async_computation.62 | async-start | bytes 2621440 | tf_op jit(solution)/shard_map/reduce_scatter | solution.py:35
  1548.1 192.5 %reduce-scatter.56.cloned.1.call-start = ((), (), s32[]{:S(2)}) async-start(), calls=%async_computation.56 | async-start | bytes 2621440 | tf_op jit(solution)/shard_map/reduce_scatter | solution.py:35
  1552.0 259.8 %reduce-scatter.90.cloned.1.call-start = ((), (), s32[]{:S(2)}) async-start(), calls=%async_computation.85 | async-start | bytes 2359296 | tf_op jit(solution)/shard_map/reduce_scatter | solution.py:40
  1608.8 269.6 %reduce-scatter.94.cloned.1.call-start = ((), (), s32[]{:S(2)}) async-start(), calls=%async_computation.87 | async-start | bytes 1179648 | tf_op jit(solution)/shard_map/reduce_scatter | solution.py:42
  1615.1 354.7 %reduce-scatter.96.cloned.1.call-start = ((), (), s32[]{:S(2)}) async-start(), calls=%async_computation.88 | async-start | bytes 4718592 | tf_op jit(solution)/shard_map/reduce_scatter | solution.py:43
  1624.7 436.9 %reduce-scatter.98.cloned.1.call-start = ((), (), s32[]{:S(2)}) async-start(), calls=%async_computation.89 | async-start | bytes 4718592 | tf_op jit(solution)/shard_map/reduce_scatter | solution.py:44
  1635.1 505.9 %reduce-scatter.92.cloned.1.call-start = ((), (), s32[]{:S(2)}) async-start(), calls=%async_computation.86 | async-start | bytes 3538944 | tf_op jit(solution)/shard_map/reduce_scatter | solution.py:41
  (234 other events, 12966.5 us)
Sparse Core Ops, SparseCore 0:
  10.7 42.8 all-gather.41
  90.8 31.4 reduce-scatter.39
  158.6 31.4 reduce-scatter.51
  192.5 45.3 all-gather.45
  313.6 37.0 all-gather.95
  599.3 31.4 reduce-scatter.47
  667.5 31.4 reduce-scatter.35
  701.1 49.2 all-gather.49
  844.6 49.2 all-gather.51
  950.2 31.4 reduce-scatter.81
  984.9 31.4 reduce-scatter.73
  1018.9 31.4 reduce-scatter.65
  1052.9 31.4 reduce-scatter.57
  1425.9 31.4 reduce-scatter.71
  1459.8 31.4 reduce-scatter.63
  1493.9 31.4 reduce-scatter.79
  1606.5 31.4 reduce-scatter.37
  1641.1 31.5 reduce-scatter.43
  1709.2 31.4 reduce-scatter.55
  1744.2 67.5 reduce-scatter.89
  1815.8 62.4 reduce-scatter.93
  1882.8 87.0 reduce-scatter.95
  1973.9 87.6 reduce-scatter.97
  2066.2 74.6 reduce-scatter.91
  (41 shorter events, 918.8 us)
where the time goes:
time: 2160 us; the launch traced here: 2150 us
  waiting for transfers between devices  1570 us (73%)
  matrix products  256 us (12%)
  blocking collectives  155 us (7%)
  other arithmetic  86.4 us (4%)
  local copies, waits for them, and re-layouts  58.5 us (3%)
    reduce_scatter x20, waiting for transfers between devices, fold_rows(): return lax.psum_scatter(block, 'tp', scatter_dimension=1, tiled=True)  519 us
    all_gather x20, waiting for transfers between devices, spread_rows(): return lax.all_gather(block, 'tp', axis=1, tiled=True)  196 us
    reduce_scatter x4, waiting for transfers between devices, micro_step(): lax.psum_scatter(key_terms.reshape(groups, seq_len, heads_dev * HD).astyp...  109 us
    all_gather x4, waiting for transfers between devices, micro_step(): lax.all_gather(project[:, :, 2], 'ctx', axis=1, tiled=True)  97.3 us
    reduce_scatter x1, waiting for transfers between devices, reduce_weights(): lax.psum_scatter(parts[4], ('fsdp', 'ctx'), scatter_dimension=0, tiled=True)  91.7 us
    reduce_scatter x1, waiting for transfers between devices, reduce_weights(): lax.psum_scatter(parts[3], ('fsdp', 'ctx'), scatter_dimension=0, tiled=True)  91.6 us
    reduce_scatter x1, waiting for transfers between devices, reduce_weights(): lax.psum_scatter(parts[1], ('fsdp', 'ctx'), scatter_dimension=0, tiled=True)  79.3 us
    unnamed x2, blocking collectives  79.3 us
  transfers between devices with their start and end apart: 65, of which 55 were waited for; matrix products, arithmetic and copies ran while one was open for 16% of the time, Pallas kernels for 0%

commit v1 on v0

--- a/solution.py
+++ b/solution.py
@@ -1,3 +1,4 @@
+import functools
 import jax
 import jax.numpy as jnp
 from jax import lax
@@ -5,6 +6,29 @@
 
 HD = 64
 EPSILON = 1e-05
+
+
+def supply_all_shifts_all(piece_in, peer_axis):
+    axis_total = jax.lax.psum(1, peer_axis)
+    n_now = map(lambda w: (w, (w + 1) % axis_total), range(axis_total))
+    line_up = list(n_now)
+    w1 = map(lambda w: (w, (w - 1) % axis_total), range(axis_total))
+    kept_arr, carry = ([piece_in], [piece_in])
+    rows = list(w1)
+    for _ in range(axis_total // 2):
+        opened = jax.lax.ppermute(kept_arr[-1], peer_axis, line_up)
+        kept_arr.append(opened)
+    for _ in range((axis_total - 1) // 2):
+        all_values = jax.lax.ppermute(carry[-1], peer_axis, rows)
+        carry.append(all_values)
+    fresh = jnp.concatenate([*kept_arr[::-1], *carry[1:]], axis=1)
+    prior = jnp.roll(
+        fresh, (jax.lax.axis_index(peer_axis) - axis_total // 2) * piece_in.shape[1], axis=1
+    )
+    return prior
+
+
+update_sources_all = functools.partial(supply_all_shifts_all, peer_axis="tp")
 
 
 def layer_norm(matrix, scales, shifts):
@@ -28,7 +52,7 @@
 
 
 def spread_rows(block):
-    return lax.all_gather(block, "tp", axis=1, tiled=True)
+    return update_sources_all(block)
 
 
 def fold_rows(block):

time: 2160 us -> 1840 us (0.85)
  waiting for transfers between devices: 1570 us -> 1170 us
  other arithmetic: 86.4 us -> 136 us
  starting transfers between devices: 4.62 us -> 49.4 us
  matrix products: 256 us -> 233 us
    all_gather x20 -> x0, waiting for transfers between devices: 196 us -> none  [spread_rows(): return lax.all_gather(block, 'tp', axis=1, tiled=True)]
    ppermute x0 -> x60, waiting for transfers between devices: none -> 163 us  [the longest x40 162 us: supply_all_shifts_all(): opened = jax.lax.ppermute(kept_arr[-1], peer_axis, line_up)]
    reduce_scatter x20, waiting for transfers between devices: 519 us -> 379 us  [fold_rows(): return lax.psum_scatter(block, 'tp', scatter_dimension=1, tiled=True)]
    reduce_scatter x4, waiting for transfers between devices: 109 us -> 44.6 us  [micro_step(): lax.psum_scatter(key_terms.reshape(groups, seq_len, heads_dev * HD).astyp...]
    ppermute x0 -> x60, starting transfers between devices: none -> 46.3 us  [the longest x20 30.3 us: supply_all_shifts_all(): all_values = jax.lax.ppermute(carry[-1], peer_axis, rows)]
    concatenate x0 -> x15, other arithmetic: none -> 45.9 us  [supply_all_shifts_all(): jnp.roll(fresh, (jax.lax.axis_index(peer_axis) - axis_total // 2) * piece...]
    all_gather x1, waiting for transfers between devices: 38.8 us -> 0.01 us  [fetch(): lax.all_gather(shrink_part, ('fsdp', 'ctx'), axis=0, tiled=True)]
    reduce_scatter x4, waiting for transfers between devices: 57 us -> 19.1 us  [micro_step(): lax.psum_scatter(value_terms.reshape(groups, seq_len, heads_dev * HD).ast...]
  transfers between devices with their start and end apart: 65 -> 105, of which waited for: 55 -> 64; matrix products, arithmetic and copies ran while one was open for 16% -> 20% of each run, Pallas kernels for 0% -> 0%
where the time goes in v1:
time: 1840 us; the launch traced here: 1830 us
  waiting for transfers between devices  1170 us (64%)
  matrix products  233 us (13%)
  blocking collectives  156 us (8%)
  other arithmetic  136 us (7%)
  local copies, waits for them, and re-layouts  68.4 us (4%)
  starting transfers between devices  49.4 us (3%)
    reduce_scatter x20, waiting for transfers between devices, fold_rows(): return lax.psum_scatter(block, 'tp', scatter_dimension=1, tiled=True)  379 us
    ppermute x40, waiting for transfers between devices, supply_all_shifts_all(): opened = jax.lax.ppermute(kept_arr[-1], peer_axis, line_up)  162 us
    reduce_scatter x1, waiting for transfers between devices, reduce_weights(): lax.psum_scatter(parts[4], ('fsdp', 'ctx'), scatter_dimension=0, tiled=True)  91.9 us
    reduce_scatter x1, waiting for transfers between devices, reduce_weights(): lax.psum_scatter(parts[3], ('fsdp', 'ctx'), scatter_dimension=0, tiled=True)  91.4 us
    unnamed x2, blocking collectives  79.4 us
    reduce_scatter x1, waiting for transfers between devices, reduce_weights(): lax.psum_scatter(parts[1], ('fsdp', 'ctx'), scatter_dimension=0, tiled=True)  79.3 us
    reduce_scatter x1, waiting for transfers between devices, reduce_weights(): lax.psum_scatter(parts[2], ('fsdp', 'ctx'), scatter_dimension=0, tiled=True)  64.6 us
    reduce_scatter x1, waiting for transfers between devices, reduce_weights(): lax.psum_scatter(parts[0], ('fsdp', 'ctx'), scatter_dimension=0, tiled=True)  60.2 us
  transfers between devices with their start and end apart: 105, of which 64 were waited for; matrix products, arithmetic and copies ran while one was open for 20% of the time, Pallas kernels for 0%

profile of v1, /device:TPU:0, one launch (start us, length us, event | category | flops | bytes accessed | tf_op | source)
XLA Modules:
  0.0 1834.1 jit_solution(9446345232508961079)
XLA Ops:
  10.6 43.0 %all-gather.22.cloned.1.call-done = bf16[1024,2,256]{2,0,1:T(8,128)(2,1)} async-done(((bf16[128,2,256]{2,0,1:T(8,128)(2,1)}), bf16[1024,2,256]{2,0,1:T(8,128)(2,1)}) %all-gather.22.cloned.1.call-update) | async-done | bytes 1048592 | tf_op jit(solution)/shard_map/all_gather | solution.py:46
  65.9 38.9 %all-reduce.16 = (f32[1024]{0:T(1024)S(1)}, f32[1024]{0:T(1024)S(1)}, f32[1024]{0:T(1024)S(1)}, f32[1024]{0:T(1024)S(1)}, f32[1024]{0:T(1024)S(1)}, /*index=5*/f32[1024]{0:T(1024)S(1)}) all-reduce(f32[1024]{0:T(1024)S(1)} %dynamic-update-slice.3, ...), channel_id=1, replica_groups=mesh['fsdp'=2,'ctx'=4,'tp'=4] {'fsdp','ctx','tp'}, use_global_device_ids=true, to_apply=%add | all-reduce | flops 6144 | bytes 49152
  122.3 33.8 %reduce-scatter.46.cloned.1.call-done = f32[2,64,1024]{2,1,0:T(8,128)} async-done(((f32[2,256,1024]{2,1,0:T(8,128)}), f32[2,64,1024]{2,1,0:T(8,128)}) %reduce-scatter.46.cloned.1.call-update) | async-done | bytes 524304 | tf_op jit(solution)/shard_map/reduce_scatter | solution.py:59
  156.1 34.0 %reduce-scatter.52.cloned.1.call-done = f32[2,64,1024]{2,1,0:T(8,128)} async-done(((f32[2,256,1024]{2,1,0:T(8,128)}), f32[2,64,1024]{2,1,0:T(8,128)}) %reduce-scatter.52.cloned.1.call-update) | async-done | bytes 524304 | tf_op jit(solution)/shard_map/reduce_scatter | solution.py:59
  210.2 27.7 %all-gather.24.cloned.1.call-done = bf16[1024,3,256]{0,2,1:T(8,128)(2,1)} async-done(((bf16[128,3,256]{0,2,1:T(8,128)(2,1)}), bf16[1024,3,256]{0,2,1:T(8,128)(2,1)}) %all-gather.24.cloned.1.call-update) | async-done | bytes 1572880 | tf_op jit(solution)/shard_map/all_gather | solution.py:47
  301.1 35.3 %all_gather.85 = bf16[1024,256]{1,0:T(8,128)(2,1)S(1)} all-gather(bf16[128,256]{1,0:T(8,128)(2,1)S(1)} %copy-done.151), channel_id=1, replica_groups=mesh['fsdp'=2,'ctx'=4,'tp'=4] {'fsdp','ctx'}, dimensions={0}, use_global_device_ids=true | all-gather | bytes 589824 | tf_op jit(solution)/shard_map/all_gather | solution.py:48
  374.8 23.4 %all-gather.44.cloned.1.call-done = bf16[2,1024,1,256]{1,3,2,0:T(8,128)(2,1)} async-done(((bf16[2,256,1,256]{1,3,2,0:T(8,128)(2,1)}), bf16[2,1024,1,256]{1,3,2,0:T(8,128)(2,1)}) %all-gather.44.cloned.1.call-update) | async-done | bytes 1048592 | tf_op jit(solution)/shard_map/all_gather | solution.py:102
  404.1 24.1 %all-gather.42.cloned.1.call-done = bf16[2,1024,1,256]{1,3,2,0:T(8,128)(2,1)} async-done(((bf16[2,256,1,256]{1,3,2,0:T(8,128)(2,1)}), bf16[2,1024,1,256]{1,3,2,0:T(8,128)(2,1)}) %all-gather.42.cloned.1.call-update) | async-done | bytes 1048592 | tf_op jit(solution)/shard_map/all_gather | solution.py:103
  464.3 24.0 %all-gather.30.cloned.1.call-done = bf16[2,1024,1,256]{1,3,2,0:T(8,128)(2,1)} async-done(((bf16[2,256,1,256]{1,3,2,0:T(8,128)(2,1)}), bf16[2,1024,1,256]{1,3,2,0:T(8,128)(2,1)}) %all-gather.30.cloned.1.call-update) | async-done | bytes 1048592 | tf_op jit(solution)/shard_map/all_gather | solution.py:103
  520.9 34.6 %reduce-scatter.48.cloned.1.call-done = f32[2,64,1024]{2,1,0:T(8,128)} async-done(((f32[2,256,1024]{2,1,0:T(8,128)}), f32[2,64,1024]{2,1,0:T(8,128)}) %reduce-scatter.48.cloned.1.call-update) | async-done | bytes 524304 | tf_op jit(solution)/shard_map/reduce_scatter | solution.py:59
  555.5 33.8 %reduce-scatter.54.cloned.1.call-done = f32[2,64,1024]{2,1,0:T(8,128)} async-done(((f32[2,256,1024]{2,1,0:T(8,128)}), f32[2,64,1024]{2,1,0:T(8,128)}) %reduce-scatter.54.cloned.1.call-update) | async-done | bytes 524304 | tf_op jit(solution)/shard_map/reduce_scatter | solution.py:59
  589.3 34.0 %reduce-scatter.36.cloned.1.call-done = f32[2,64,1024]{2,1,0:T(8,128)} async-done(((f32[2,256,1024]{2,1,0:T(8,128)}), f32[2,64,1024]{2,1,0:T(8,128)}) %reduce-scatter.36.cloned.1.call-update) | async-done | bytes 524304 | tf_op jit(solution)/shard_map/reduce_scatter | solution.py:59
  629.6 41.6 %all-gather.8 = f32[32,1,128]{2,1,0:T(1,128)S(1)} all-gather(f32[1,1,128]{2,1,0:T(1,128)S(1)} %bitcast.619), channel_id=1, replica_groups=mesh['fsdp'=2,'ctx'=4,'tp'=4] {'fsdp','ctx','tp'}, dimensions={0}, use_global_device_ids=true | all-gather | bytes 16896 | tf_op jit(solution)/shard_map/all_gather | solution.py:278
  856.3 34.0 %reduce-scatter.58.cloned.1.call-done = f32[2,64,1024]{2,1,0:T(8,128)} async-done(((f32[2,256,1024]{2,1,0:T(8,128)}), f32[2,64,1024]{2,1,0:T(8,128)}) %reduce-scatter.58.cloned.1.call-update) | async-done | bytes 524304 | tf_op jit(solution)/shard_map/reduce_scatter | solution.py:59
  1115.9 28.2 %reduce-scatter.76.cloned.1.call-done = bf16[2,256,256]{2,1,0:T(8,128)(2,1)} async-done(((bf16[2,1024,256]{2,1,0:T(8,128)(2,1)}), bf16[2,256,256]{2,1,0:T(8,128)(2,1)}) %reduce-scatter.76.cloned.1.call-update) | async-done | bytes 262160 | tf_op jit(solution)/shard_map/reduce_scatter | solution.py:196
  1177.2 34.1 %reduce-scatter.72.cloned.1.call-done = f32[2,64,1024]{2,1,0:T(8,128)} async-done(((f32[2,256,1024]{2,1,0:T(8,128)}), f32[2,64,1024]{2,1,0:T(8,128)}) %reduce-scatter.72.cloned.1.call-update) | async-done | bytes 524304 | tf_op jit(solution)/shard_map/reduce_scatter | solution.py:59
  1211.3 34.0 %reduce-scatter.64.cloned.1.call-done = f32[2,64,1024]{2,1,0:T(8,128)} async-done(((f32[2,256,1024]{2,1,0:T(8,128)}), f32[2,64,1024]{2,1,0:T(8,128)}) %reduce-scatter.64.cloned.1.call-update) | async-done | bytes 524304 | tf_op jit(solution)/shard_map/reduce_scatter | solution.py:59
  1245.3 34.0 %reduce-scatter.80.cloned.1.call-done = f32[2,64,1024]{2,1,0:T(8,128)} async-done(((f32[2,256,1024]{2,1,0:T(8,128)}), f32[2,64,1024]{2,1,0:T(8,128)}) %reduce-scatter.80.cloned.1.call-update) | async-done | bytes 524304 | tf_op jit(solution)/shard_map/reduce_scatter | solution.py:59
  1374.5 40.5 %all-reduce.15 = (f32[1024]{0:T(1024)S(1)}, f32[1024]{0:T(1024)S(1)}, f32[1024]{0:T(1024)S(1)}, f32[1024]{0:T(1024)S(1)}, f32[1024]{0:T(1024)S(1)}, /*index=5*/f...) all-reduce(f32[1024]{0:T(1024)S(1)} %dynamic-update-slice.9, ...), channel_id=1, replica_groups=mesh['fsdp'=2,'ctx'=4,'tp'=4] {'fsdp','ctx','tp'}, use_global_device_ids=true, to_apply=%add.6 | all-reduce | flops 12288 | bytes 98304
  1437.8 60.2 %reduce-scatter.90.cloned.1.call-done = f32[128,2,256]{2,0,1:T(8,128)} async-done(((f32[1024,2,256]{2,0,1:T(8,128)}), f32[128,2,256]{2,0,1:T(8,128)}) %reduce-scatter.90.cloned.1.call-update) | async-done | bytes 262160 | tf_op jit(solution)/shard_map/reduce_scatter | solution.py:64
  1499.9 64.6 %reduce-scatter.94.cloned.1.call-done = f32[128,256]{1,0:T(8,128)} async-done(((f32[1024,256]{1,0:T(8,128)}), f32[128,256]{1,0:T(8,128)}) %reduce-scatter.94.cloned.1.call-update) | async-done | bytes 131088 | tf_op jit(solution)/shard_map/reduce_scatter | solution.py:66
  1564.5 91.4 %reduce-scatter.96.cloned.1.call-done = f32[128,1024]{1,0:T(8,128)} async-done(((f32[1024,1024]{1,0:T(8,128)}), f32[128,1024]{1,0:T(8,128)}) %reduce-scatter.96.cloned.1.call-update) | async-done | bytes 524304 | tf_op jit(solution)/shard_map/reduce_scatter | solution.py:67
  1655.9 91.9 %reduce-scatter.98.cloned.1.call-done = f32[128,1024]{1,0:T(8,128)} async-done(((f32[1024,1024]{1,0:T(8,128)}), f32[128,1024]{1,0:T(8,128)}) %reduce-scatter.98.cloned.1.call-update) | async-done | bytes 524304 | tf_op jit(solution)/shard_map/reduce_scatter | solution.py:68
  1747.8 79.3 %reduce-scatter.92.cloned.1.call-done = f32[128,3,256]{2,0,1:T(8,128)} async-done(((f32[1024,3,256]{2,0,1:T(8,128)}), f32[128,3,256]{2,0,1:T(8,128)}) %reduce-scatter.92.cloned.1.call-update) | async-done | bytes 393232 | tf_op jit(solution)/shard_map/reduce_scatter | solution.py:65
  (927 shorter events, 795.4 us)
Async XLA Ops:
  63.6 174.3 %all-gather.24.cloned.1.call-start = ((), (), s32[]{:S(2)}) async-start(), calls=%async_computation.35 | async-start | bytes 1769472 | tf_op jit(solution)/shard_map/all_gather | solution.py:47
  64.5 272.0 %all-gather.36.cloned.1.call-start = ((), (), s32[]{:S(2)}) async-start(), calls=%async_computation.73 | async-start | bytes 1310720 | tf_op jit(solution)/shard_map/all_gather | solution.py:102
  280.5 177.8 %all-gather.32.cloned.1.call-start = ((), (), s32[]{:S(2)}) async-start(), calls=%async_computation.71 | async-start | bytes 1310720 | tf_op jit(solution)/shard_map/all_gather | solution.py:102
  301.1 187.2 %all-gather.30.cloned.1.call-start = ((), (), s32[]{:S(2)}) async-start(), calls=%async_computation.70 | async-start | bytes 1310720 | tf_op jit(solution)/shard_map/all_gather | solution.py:103
  336.4 184.5 %reduce-scatter.42.cloned.1.call-start = ((), (), s32[]{:S(2)}) async-start(), calls=%async_computation.41 | async-start | bytes 2621440 | tf_op jit(solution)/shard_map/reduce_scatter | solution.py:59
  349.9 205.7 %reduce-scatter.48.cloned.1.call-start = ((), (), s32[]{:S(2)}) async-start(), calls=%async_computation.44 | async-start | bytes 2621440 | tf_op jit(solution)/shard_map/reduce_scatter | solution.py:59
  374.8 214.6 %reduce-scatter.54.cloned.1.call-start = ((), (), s32[]{:S(2)}) async-start(), calls=%async_computation.47 | async-start | bytes 2621440 | tf_op jit(solution)/shard_map/reduce_scatter | solution.py:59
  435.4 188.0 %reduce-scatter.36.cloned.1.call-start = ((), (), s32[]{:S(2)}) async-start(), calls=%async_computation.36 | async-start | bytes 2621440 | tf_op jit(solution)/shard_map/reduce_scatter | solution.py:59
  495.5 193.6 %all-gather.26.cloned.1.call-start = ((), (), s32[]{:S(2)}) async-start(), calls=%async_computation.37 | async-start | bytes 2359296 | tf_op jit(solution)/shard_map/all_gather | solution.py:49
  496.2 243.0 %all-gather.28.cloned.1.call-start = ((), (), s32[]{:S(2)}) async-start(), calls=%async_computation.38 | async-start | bytes 2359296 | tf_op jit(solution)/shard_map/all_gather | solution.py:50
  629.6 204.4 %reduce-scatter.82.cloned.1.call-start = ((), (), s32[]{:S(2)}) async-start(), calls=%async_computation.61 | async-start | bytes 2621440 | tf_op jit(solution)/shard_map/reduce_scatter | solution.py:59
  833.9 219.0 %reduce-scatter.86.cloned.1.call-start = ((), (), s32[]{:S(2)}) async-start(), calls=%async_computation.63 | async-start | bytes 1310720 | tf_op jit(solution)/shard_map/reduce_scatter | solution.py:202
  1057.5 153.9 %reduce-scatter.72.cloned.1.call-start = ((), (), s32[]{:S(2)}) async-start(), calls=%async_computation.56 | async-start | bytes 2621440 | tf_op jit(solution)/shard_map/reduce_scatter | solution.py:59
  1066.4 178.9 %reduce-scatter.64.cloned.1.call-start = ((), (), s32[]{:S(2)}) async-start(), calls=%async_computation.52 | async-start | bytes 2621440 | tf_op jit(solution)/shard_map/reduce_scatter | solution.py:59
  1091.8 187.5 %reduce-scatter.80.cloned.1.call-start = ((), (), s32[]{:S(2)}) async-start(), calls=%async_computation.60 | async-start | bytes 2621440 | tf_op jit(solution)/shard_map/reduce_scatter | solution.py:59
  1148.0 271.6 %reduce-scatter.38.cloned.1.call-start = ((), (), s32[]{:S(2)}) async-start(), calls=%async_computation.39 | async-start | bytes 2621440 | tf_op jit(solution)/shard_map/reduce_scatter | solution.py:59
  1153.5 266.2 %reduce-scatter.44.cloned.1.call-start = ((), (), s32[]{:S(2)}) async-start(), calls=%async_computation.42 | async-start | bytes 2621440 | tf_op jit(solution)/shard_map/reduce_scatter | solution.py:59
  1159.0 260.6 %reduce-scatter.50.cloned.1.call-start = ((), (), s32[]{:S(2)}) async-start(), calls=%async_computation.45 | async-start | bytes 2621440 | tf_op jit(solution)/shard_map/reduce_scatter | solution.py:59
  1164.4 262.0 %reduce-scatter.56.cloned.1.call-start = ((), (), s32[]{:S(2)}) async-start(), calls=%async_computation.48 | async-start | bytes 2621440 | tf_op jit(solution)/shard_map/reduce_scatter | solution.py:59
  1170.0 328.1 %reduce-scatter.90.cloned.1.call-start = ((), (), s32[]{:S(2)}) async-start(), calls=%async_computation.65 | async-start | bytes 2359296 | tf_op jit(solution)/shard_map/reduce_scatter | solution.py:64
  1339.0 225.5 %reduce-scatter.94.cloned.1.call-start = ((), (), s32[]{:S(2)}) async-start(), calls=%async_computation.67 | async-start | bytes 1179648 | tf_op jit(solution)/shard_map/reduce_scatter | solution.py:66
  1344.5 311.5 %reduce-scatter.96.cloned.1.call-start = ((), (), s32[]{:S(2)}) async-start(), calls=%async_computation.68 | async-start | bytes 4718592 | tf_op jit(solution)/shard_map/reduce_scatter | solution.py:67
  1353.1 394.7 %reduce-scatter.98.cloned.1.call-start = ((), (), s32[]{:S(2)}) async-start(), calls=%async_computation.69 | async-start | bytes 4718592 | tf_op jit(solution)/shard_map/reduce_scatter | solution.py:68
  1363.7 463.4 %reduce-scatter.92.cloned.1.call-start = ((), (), s32[]{:S(2)}) async-start(), calls=%async_computation.66 | async-start | bytes 3538944 | tf_op jit(solution)/shard_map/reduce_scatter | solution.py:65
  (308 other events, 10461.4 us)
Sparse Core Ops, SparseCore 0:
  10.7 42.8 all-gather.21
  90.8 31.4 reduce-scatter.39
  124.6 31.4 reduce-scatter.45
  158.6 31.3 reduce-scatter.51
  192.5 45.3 all-gather.23
  302.5 34.9 all-gather.39
  524.1 31.4 reduce-scatter.47
  591.9 31.4 reduce-scatter.35
  625.5 49.2 all-gather.25
  676.7 47.7 all-gather.27
  779.9 41.5 reduce-scatter.73
  824.0 32.1 reduce-scatter.65
  858.8 31.4 reduce-scatter.57
  1179.9 31.3 reduce-scatter.71
  1213.9 31.4 reduce-scatter.63
  1247.9 31.3 reduce-scatter.79
  1282.3 40.7 reduce-scatter.37
  1325.7 32.0 reduce-scatter.43
  1360.2 32.1 reduce-scatter.49
  1429.9 68.0 reduce-scatter.89
  1502.0 62.4 reduce-scatter.93
  1569.0 86.8 reduce-scatter.95
  1660.1 87.6 reduce-scatter.97
  1752.3 74.7 reduce-scatter.91
  (21 shorter events, 585.8 us)
